TPU v7x, 32 devices: a whole 2x2x4 slice. The times are simulated.
32 devices in a mesh: dp: 8 (over y, x, core), mp: 4 (over z).
Axes of the slice: x: 2, y: 2, z: 4, core: 2. Of those that a mesh axis runs over, the one named last changes fastest.
Arguments:
- patches: bfloat16 [8192, 768], P('dp'), may hold values from -6 to 6
- attention_gain: bfloat16 [768], replicated, may hold values from 0.5 to 1.5
- query_weight: bfloat16 [768, 768], P(None, 'mp'), may hold values from -0.0390625 to 0.0390625
- key_weight: bfloat16 [768, 768], P(None, 'mp'), may hold values from -0.3125 to 0.3125
- value_weight: bfloat16 [768, 768], P(None, 'mp'), may hold values from -0.21875 to 0.21875
- output_weight: bfloat16 [768, 768], P('mp'), may hold values from -0.875 to 0.875
- feedforward_gain: bfloat16 [768], replicated, may hold values from 0.5 to 1.5
- gate_weight: bfloat16 [768, 2048], P(None, 'mp'), may hold values from -0.21875 to 0.21875
- up_weight: bfloat16 [768, 2048], P(None, 'mp'), may hold values from -0.21875 to 0.21875
- down_weight: bfloat16 [2048, 768], P('mp'), may hold values from -0.25 to 0.25
- cotangent: bfloat16 [8192, 768], P('dp'), may hold values from -6 to 6
- grid_extent: int32 [8, 2], P('dp'), may hold values from 16 to 32, as said below
Outputs:
- layer_output: bfloat16 [8192, 768], P('dp')
- input_grad: float32 [8192, 768], P('dp')
- attention_grad: float32 [768], P('dp')
- query_grad: float32 [768, 768], P('dp', 'mp')
- key_grad: float32 [768, 768], P('dp', 'mp')
- value_grad: float32 [768, 768], P('dp', 'mp')
- output_grad: float32 [768, 768], P('mp', 'dp')
- feedforward_grad: float32 [768], P('dp')
- gate_grad: float32 [768, 2048], P('dp', 'mp')
- up_grad: float32 [768, 2048], P('dp', 'mp')
- down_grad: float32 [2048, 768], P('mp', 'dp')
Inputs may be any that keep to these rules, and one draw needn't show every extreme that they name: `grid_extent`: chart 0 has all 32 rows and columns.
All inputs are finite; a program needn't handle non-finite values.
Results may differ from a plain program's by a relative error of at most 0.015.
Values may be sent and summed in bfloat16 or wider, within the bound.
A program may use at most 128 MiB of HBM per device.

v0:
```python
import jax
import jax.numpy as jnp
from jax import lax
from jax.sharding import PartitionSpec as P

HEAD = 64
epsilon = 1e-06
masked_score = -1000000000.0


def rms_scale(values, gain_vec):
    return (
        values * lax.rsqrt(jnp.mean(values * values, axis=-1, keepdims=True) + epsilon) * gain_vec
    )


def patch_valid(grid_extent, length):
    position = jnp.arange(length, dtype=jnp.int32)
    return position[None, :] < grid_extent[:, 0:1] * grid_extent[:, 1:2]


def query_blocks(length):
    block_rows = min(512, length)
    return (block_rows, jnp.arange(length // block_rows, dtype=jnp.int32) * block_rows)


def block_scores(query_block, keys_all, key_bias):
    scores = jnp.einsum("qhd,khd->hqk", query_block, keys_all, preferred_element_type=jnp.float32)
    return scores + key_bias


def attend_chart(chart_item):
    queries, keys_all, values_all, key_ok = chart_item
    block_rows, starts = query_blocks(queries.shape[0])
    key_bias = jnp.where(key_ok, 0.0, masked_score).astype(jnp.float32)

    def one_block(start):
        query_block = lax.dynamic_slice_in_dim(queries, start, block_rows, 0)
        scores = block_scores(query_block, keys_all, key_bias)
        highest = jnp.max(scores, axis=-1, keepdims=True)
        logsum = highest + jnp.log(jnp.sum(jnp.exp(scores - highest), axis=-1, keepdims=True))
        probs = jnp.exp(scores - logsum).astype(jnp.bfloat16)
        context = jnp.einsum("hqk,khd->qhd", probs, values_all, preferred_element_type=jnp.float32)
        return (context.astype(jnp.bfloat16), logsum)

    context, logsum = lax.map(one_block, starts)
    return (context.reshape(queries.shape), logsum)


def attend_back(chart_item):
    queries, keys_all, values_all, key_ok, logsum, context_back = chart_item
    block_rows, starts = query_blocks(queries.shape[0])
    key_bias = jnp.where(key_ok, 0.0, masked_score).astype(jnp.float32)

    def one_block(carry, block_item):
        key_total, value_total = carry
        start, block_logsum = block_item
        query_block = lax.dynamic_slice_in_dim(queries, start, block_rows, 0)
        grad_block = lax.dynamic_slice_in_dim(context_back, start, block_rows, 0)
        probs_full = jnp.exp(block_scores(query_block, keys_all, key_bias) - block_logsum)
        value_total = value_total + jnp.einsum(
            "hqk,qhd->khd",
            probs_full.astype(jnp.bfloat16),
            grad_block,
            preferred_element_type=jnp.float32,
        )
        probs_back = jnp.einsum(
            "qhd,khd->hqk", grad_block, values_all, preferred_element_type=jnp.float32
        )
        score_back = probs_full * (
            probs_back - jnp.sum(probs_full * probs_back, axis=-1, keepdims=True)
        )
        score_back = score_back.astype(jnp.bfloat16)
        query_part = jnp.einsum(
            "hqk,khd->qhd", score_back, keys_all, preferred_element_type=jnp.float32
        )
        key_total = key_total + jnp.einsum(
            "hqk,qhd->khd", score_back, query_block, preferred_element_type=jnp.float32
        )
        return ((key_total, value_total), query_part.astype(jnp.bfloat16))

    zeros_keys = jnp.zeros(keys_all.shape, jnp.float32)
    (key_total, value_total), query_back = lax.scan(
        one_block, (zeros_keys, zeros_keys), (starts, logsum)
    )
    return (
        query_back.reshape(queries.shape),
        key_total.astype(jnp.bfloat16),
        value_total.astype(jnp.bfloat16),
    )


def layer_forward(inputs, weights, valid_mask, attention_total):
    (
        first_gain,
        query_weight,
        key_weight,
        value_weight,
        output_weight,
        second_gain,
        gate_weight,
        up_weight,
        down_weight,
    ) = weights
    rows_total = inputs.shape[0]
    charts = valid_mask.shape[0]
    length = rows_total // charts
    normed_one = rms_scale(inputs, first_gain).astype(jnp.bfloat16)

    def project(matrix):
        product = jnp.dot(normed_one, matrix, preferred_element_type=jnp.float32)
        return product.astype(jnp.bfloat16).reshape(charts, length, matrix.shape[1] // HEAD, HEAD)

    queries = project(query_weight)
    keys_all = project(key_weight)
    values_all = project(value_weight)
    context, logsum = lax.map(attend_chart, (queries, keys_all, values_all, valid_mask))
    context = context.reshape(rows_total, query_weight.shape[1])
    attention_out = attention_total(
        jnp.dot(context, output_weight, preferred_element_type=jnp.float32)
    )
    hidden = inputs + attention_out
    normed_two = rms_scale(hidden, second_gain).astype(jnp.bfloat16)
    gate_pre = jnp.dot(normed_two, gate_weight, preferred_element_type=jnp.float32)
    up_pre = jnp.dot(normed_two, up_weight, preferred_element_type=jnp.float32)
    mixed = (jax.nn.gelu(gate_pre, approximate=True) * up_pre).astype(jnp.bfloat16)
    return (
        normed_one,
        queries,
        keys_all,
        values_all,
        logsum,
        context,
        hidden,
        normed_two,
        gate_pre,
        up_pre,
        mixed,
    )


def gelu_product(gate_pre, up_pre):
    return jax.nn.gelu(gate_pre, approximate=True) * up_pre


def body(
    patches,
    attention_gain,
    query_weight,
    key_weight,
    value_weight,
    output_weight,
    feedforward_gain,
    gate_weight,
    up_weight,
    down_weight,
    cotangent,
    grid_extent,
):
    rows_total = patches.shape[0]
    charts = grid_extent.shape[0]
    length = rows_total // charts
    valid_mask = patch_valid(grid_extent, length)
    row_keep = valid_mask.reshape(rows_total, 1)
    inputs = patches.astype(jnp.float32)
    first_gain = attention_gain.astype(jnp.float32)
    second_gain = feedforward_gain.astype(jnp.float32)
    weights = (
        first_gain,
        query_weight,
        key_weight,
        value_weight,
        output_weight,
        second_gain,
        gate_weight,
        up_weight,
        down_weight,
    )

    def attention_total(partial_value):
        share = lax.psum_scatter(partial_value, "mp", scatter_dimension=0, tiled=True)
        return lax.all_gather(share, "mp", axis=0, tiled=True)

    def attention_repeat(partial_value):
        share = lax.psum_scatter(partial_value, "mp", scatter_dimension=0, tiled=True)
        return lax.all_gather(share, "mp", axis=0, tiled=True)

    first_pass = layer_forward(inputs, weights, valid_mask, attention_total)
    feedforward_share = lax.psum_scatter(
        jnp.dot(first_pass[10], down_weight, preferred_element_type=jnp.float32),
        "mp",
        scatter_dimension=0,
        tiled=True,
    )
    rows_here = feedforward_share.shape[0]
    row_start = lax.axis_index("mp") * rows_here
    hidden_here = lax.dynamic_slice_in_dim(first_pass[6], row_start, rows_here, 0)
    keep_here = lax.dynamic_slice_in_dim(row_keep, row_start, rows_here, 0)
    output_here = jnp.where(keep_here, hidden_here + feedforward_share, 0.0).astype(jnp.bfloat16)
    layer_output = lax.all_gather(output_here, "mp", axis=0, tiled=True)
    saved = layer_forward(inputs, weights, valid_mask, attention_repeat)
    (
        normed_one,
        queries,
        keys_all,
        values_all,
        logsum,
        context,
        hidden,
        normed_two,
        gate_pre,
        up_pre,
        mixed,
    ) = saved
    out_back = jnp.where(row_keep, cotangent.astype(jnp.float32), 0.0)
    out_low = out_back.astype(jnp.bfloat16)
    down_grad = jnp.einsum("rf,rd->fd", mixed, out_low, preferred_element_type=jnp.float32)
    mixed_back = jnp.einsum("rd,fd->rf", out_low, down_weight, preferred_element_type=jnp.float32)
    _, gelu_pull = jax.vjp(gelu_product, gate_pre, up_pre)
    gate_back, up_back = gelu_pull(mixed_back)
    gate_back = gate_back.astype(jnp.bfloat16)
    up_back = up_back.astype(jnp.bfloat16)
    gate_grad = jnp.einsum("rd,rf->df", normed_two, gate_back, preferred_element_type=jnp.float32)
    up_grad = jnp.einsum("rd,rf->df", normed_two, up_back, preferred_element_type=jnp.float32)
    normed_two_part = jnp.einsum(
        "rf,df->rd", gate_back, gate_weight, preferred_element_type=jnp.float32
    ) + jnp.einsum("rf,df->rd", up_back, up_weight, preferred_element_type=jnp.float32)
    normed_two_share = lax.psum_scatter(normed_two_part, "mp", scatter_dimension=0, tiled=True)
    normed_two_back = lax.all_gather(normed_two_share, "mp", axis=0, tiled=True)
    _, second_pull = jax.vjp(rms_scale, hidden, second_gain)
    hidden_part, second_gain_grad = second_pull(normed_two_back)
    hidden_back = out_back + hidden_part
    second_gain_grad, gate_grad, up_grad = (
        lax.psum_scatter(second_gain_grad, "dp", scatter_dimension=0, tiled=True),
        lax.psum_scatter(gate_grad, "dp", scatter_dimension=0, tiled=True),
        lax.psum_scatter(up_grad, "dp", scatter_dimension=0, tiled=True),
    )
    down_grad = lax.psum_scatter(down_grad, "dp", scatter_dimension=1, tiled=True)
    hidden_low = hidden_back.astype(jnp.bfloat16)
    output_grad = jnp.einsum("rc,rd->cd", context, hidden_low, preferred_element_type=jnp.float32)
    context_back = jnp.einsum(
        "rd,cd->rc", hidden_low, output_weight, preferred_element_type=jnp.float32
    )
    context_back = context_back.astype(jnp.bfloat16).reshape(queries.shape)
    query_back, key_back, value_back = lax.map(
        attend_back, (queries, keys_all, values_all, valid_mask, logsum, context_back)
    )
    features_here = query_weight.shape[1]
    query_back = query_back.reshape(rows_total, features_here)
    key_back = key_back.reshape(rows_total, features_here)
    value_back = value_back.reshape(rows_total, features_here)
    query_grad = jnp.einsum("rd,rc->dc", normed_one, query_back, preferred_element_type=jnp.float32)
    key_grad = jnp.einsum("rd,rc->dc", normed_one, key_back, preferred_element_type=jnp.float32)
    value_grad = jnp.einsum("rd,rc->dc", normed_one, value_back, preferred_element_type=jnp.float32)
    normed_one_part = (
        jnp.einsum("rc,dc->rd", query_back, query_weight, preferred_element_type=jnp.float32)
        + jnp.einsum("rc,dc->rd", key_back, key_weight, preferred_element_type=jnp.float32)
        + jnp.einsum("rc,dc->rd", value_back, value_weight, preferred_element_type=jnp.float32)
    )
    normed_one_share = lax.psum_scatter(normed_one_part, "mp", scatter_dimension=0, tiled=True)
    normed_one_back = lax.all_gather(normed_one_share, "mp", axis=0, tiled=True)
    _, first_pull = jax.vjp(rms_scale, inputs, first_gain)
    input_part, first_gain_grad = first_pull(normed_one_back)
    input_grad = hidden_back + input_part
    first_gain_grad, query_grad, key_grad, value_grad = (
        lax.psum_scatter(first_gain_grad, "dp", scatter_dimension=0, tiled=True),
        lax.psum_scatter(query_grad, "dp", scatter_dimension=0, tiled=True),
        lax.psum_scatter(key_grad, "dp", scatter_dimension=0, tiled=True),
        lax.psum_scatter(value_grad, "dp", scatter_dimension=0, tiled=True),
    )
    output_grad = lax.psum_scatter(output_grad, "dp", scatter_dimension=1, tiled=True)
    return (
        layer_output,
        input_grad,
        first_gain_grad,
        query_grad,
        key_grad,
        value_grad,
        output_grad,
        second_gain_grad,
        gate_grad,
        up_grad,
        down_grad,
    )


def solution(mesh):
    placed = (
        P("dp", None),
        P(),
        P(None, "mp"),
        P(None, "mp"),
        P(None, "mp"),
        P("mp", None),
        P(),
        P(None, "mp"),
        P(None, "mp"),
        P("mp", None),
        P("dp", None),
        P("dp", None),
    )
    return jax.shard_map(
        body,
        mesh=mesh,
        in_specs=placed,
        out_specs=(
            P("dp", None),
            P("dp", None),
            P("dp"),
            P("dp", "mp"),
            P("dp", "mp"),
            P("dp", "mp"),
            P("mp", "dp"),
            P("dp"),
            P("dp", "mp"),
            P("dp", "mp"),
            P("mp", "dp"),
        ),
        check_vma=False,
    )
```

profile of v0, /device:TPU:0, one launch (start us, length us, event | category | flops | bytes accessed | tf_op | source)
XLA Modules:
  0.0 994.6 jit_solution(6283610246792495754)
XLA Ops:
  16.5 12.8 %while.67 = (s32[]{:T(128)}, bf16[2,512,3,64]{1,3,2,0:T(8,128)(2,1)S(1)}, f32[2,3,512,1]{2,1,3,0:T(4,128)S(1)}, s32[2]{0:T(128)S(1)}, bf16[1024,3,64]{0,2,1:T(8,...) while((s32[]{:T(128)}, ...), condition=%wide.region_11.12_spmd.clone, body=%wide.region_8.11_spmd.clone.sunk | while | flops 415334912 | bytes 20129972 | solution.py:46
  33.3 63.0 %reduce-scatter.19.cloned.1.call-done = f32[256,768]{1,0:T(8,128)} async-done(((f32[1024,768]{1,0:T(8,128)}), f32[256,768]{1,0:T(8,128)}) %reduce-scatter.19.cloned.1.call-update) | async-done | bytes 786448 | tf_op jit(solution)/shard_map/reduce_scatter | solution.py:185
  96.5 65.0 %all-gather.10.cloned.1.call-done = f32[1024,768]{1,0:T(8,128)} async-done(((f32[256,768]{1,0:T(8,128)}), f32[1024,768]{1,0:T(8,128)}) %all-gather.10.cloned.1.call-update) | async-done | bytes 3145744 | tf_op jit(solution)/shard_map/all_gather | solution.py:186
  175.9 59.0 %reduce-scatter.21.cloned.1.call-done = f32[256,768]{1,0:T(8,128)} async-done(((f32[1024,768]{1,0:T(8,128)}), f32[256,768]{1,0:T(8,128)}) %reduce-scatter.21.cloned.1.call-update) | async-done | bytes 786448 | tf_op jit(solution)/shard_map/reduce_scatter | solution.py:228
  235.5 64.4 %all-gather.12.cloned.1.call-done = f32[1024,768]{1,0:T(8,128)} async-done(((f32[256,768]{1,0:T(8,128)}), f32[1024,768]{1,0:T(8,128)}) %all-gather.12.cloned.1.call-update) | async-done | bytes 3145744 | tf_op jit(solution)/shard_map/all_gather | solution.py:229
  310.5 24.8 %while.68 = (s32[]{:T(128)}, f32[1024,3,64]{0,2,1:T(8,128)S(1)}, f32[1024,3,64]{0,2,1:T(8,128)}, bf16[2,512,3,64]{1,3,2,0:T(8,128)(2,1)}, s32[2]{0:T(128)}, /*in...) while((s32[]{:T(128)}, f32[1024,3,64]{0,2,1:T(8,128)S(1)}, ...), condition=%wide.region_18.19_spmd.clone, body=%wide.region_16.18_spmd.clone.sunk | while | flops 1026392576 | bytes 66714016 | solution.py:83
  342.1 14.3 %while.66 = (s32[]{:T(128)}, bf16[2,512,3,64]{1,3,2,0:T(8,128)(2,1)}, s32[2]{0:T(128)S(1)}, bf16[1024,3,64]{0,2,1:T(8,128)(2,1)S(1)}, bf16[1024,3,64]{0,2,1:T(8,...) while((s32[]{:T(128)}, ...), condition=%wide.region_4.5_spmd.clone, body=%wide.region_1.4_spmd.clone.sunk | while | flops 415334912 | bytes 23261408 | solution.py:46
  361.2 38.9 %reduce-scatter.23.cloned.1.call-done = f32[256,768]{1,0:T(8,128)} async-done(((f32[1024,768]{1,0:T(8,128)}), f32[256,768]{1,0:T(8,128)}) %reduce-scatter.23.cloned.1.call-update) | async-done | bytes 786448 | tf_op jit(solution)/shard_map/reduce_scatter | solution.py:260
  400.2 63.0 %reduce-scatter.15.cloned.1.call-done = f32[256,768]{1,0:T(8,128)} async-done(((f32[1024,768]{1,0:T(8,128)}), f32[256,768]{1,0:T(8,128)}) %reduce-scatter.15.cloned.1.call-update) | async-done | bytes 786448 | tf_op jit(solution)/shard_map/reduce_scatter | solution.py:181
  463.2 65.1 %all-gather.14.cloned.1.call-done = f32[1024,768]{1,0:T(8,128)} async-done(((f32[256,768]{1,0:T(8,128)}), f32[1024,768]{1,0:T(8,128)}) %all-gather.14.cloned.1.call-update) | async-done | bytes 3145744 | tf_op jit(solution)/shard_map/all_gather | solution.py:261
  531.3 60.7 %all-gather.6.cloned.1.call-done = f32[1024,768]{1,0:T(8,128)} async-done(((f32[256,768]{1,0:T(8,128)}), f32[1024,768]{1,0:T(8,128)}) %all-gather.6.cloned.1.call-update) | async-done | bytes 3145744 | tf_op jit(solution)/shard_map/all_gather | solution.py:182
  592.0 5.6 multiply_reduce_fusion.4
  601.7 6.3 fusion.72
  612.6 54.5 %reduce-scatter.17.cloned.1.call-done = f32[256,768]{1,0:T(8,128)} async-done(((f32[1024,768]{1,0:T(8,128)}), f32[256,768]{1,0:T(8,128)}) %reduce-scatter.17.cloned.1.call-update) | async-done | bytes 786448 | tf_op jit(solution)/shard_map/reduce_scatter | solution.py:189
  669.6 5.5 fusion.73
  688.8 16.3 %reduce-scatter.37.cloned.1.call-done = f32[96,192]{1,0:T(8,128)} async-done(((f32[768,192]{1,0:T(8,128)}), f32[96,192]{1,0:T(8,128)}) %reduce-scatter.37.cloned.1.call-update) | async-done | bytes 73744
  706.7 12.6 %all-reduce.2 = (f32[768]{0:T(1024)S(1)}, f32[768]{0:T(1024)S(1)}) all-reduce(f32[768]{0:T(1024)S(1)} %get-tuple-element.302, f32[768]{0:T(1024)S(1)} %copy-done.60), channel_id=7, replica_groups=mesh['dp'=8,'mp'=4] {'dp'}, use_global_device_ids=true, to_apply=%region_22.23.clone | all-reduce | flops 1536 | bytes 12288
  720.5 23.3 %all-gather.8.cloned.1.call-done = bf16[1024,768]{1,0:T(8,128)(2,1)} async-done(((bf16[256,768]{1,0:T(8,128)(2,1)}), bf16[1024,768]{1,0:T(8,128)(2,1)}) %all-gather.8.cloned.1.call-update) | async-done | bytes 1572880 | tf_op jit(solution)/shard_map/all_gather | solution.py:200
  743.8 41.1 %reduce-scatter.35.cloned.1.call-done = f32[512,96]{0,1:T(8,128)} async-done(((f32[512,768]{0,1:T(8,128)}), f32[512,96]{0,1:T(8,128)}) %reduce-scatter.35.cloned.1.call-update) | async-done | bytes 196624 | tf_op jit(solution)/shard_map/reduce_scatter | solution.py:238
  784.9 42.4 %reduce-scatter.31.cloned.1.call-done = f32[96,512]{1,0:T(8,128)} async-done(((f32[768,512]{1,0:T(8,128)}), f32[96,512]{1,0:T(8,128)}) %reduce-scatter.31.cloned.1.call-update) | async-done | bytes 196624 | tf_op jit(solution)/shard_map/reduce_scatter | solution.py:235
  827.2 42.2 %reduce-scatter.33.cloned.1.call-done = f32[96,512]{1,0:T(8,128)} async-done(((f32[768,512]{1,0:T(8,128)}), f32[96,512]{1,0:T(8,128)}) %reduce-scatter.33.cloned.1.call-update) | async-done | bytes 196624 | tf_op jit(solution)/shard_map/reduce_scatter | solution.py:236
  869.5 38.6 %reduce-scatter.29.cloned.1.call-done = f32[96,192]{1,0:T(8,128)} async-done(((f32[768,192]{1,0:T(8,128)}), f32[96,192]{1,0:T(8,128)}) %reduce-scatter.29.cloned.1.call-update) | async-done | bytes 73744 | tf_op jit(solution)/shard_map/reduce_scatter | solution.py:269
  908.0 38.6 %reduce-scatter.25.cloned.1.call-done = f32[96,192]{1,0:T(8,128)} async-done(((f32[768,192]{1,0:T(8,128)}), f32[96,192]{1,0:T(8,128)}) %reduce-scatter.25.cloned.1.call-update) | async-done | bytes 73744 | tf_op jit(solution)/shard_map/reduce_scatter | solution.py:267
  946.6 38.6 %reduce-scatter.27.cloned.1.call-done = f32[96,192]{1,0:T(8,128)} async-done(((f32[768,192]{1,0:T(8,128)}), f32[96,192]{1,0:T(8,128)}) %reduce-scatter.27.cloned.1.call-update) | async-done | bytes 73744 | tf_op jit(solution)/shard_map/reduce_scatter | solution.py:268
  (297 shorter events, 120.9 us)
Async XLA Ops:
  7.2 159.5 %copy-start = (bf16[768,512]{1,0:T(8,128)(2,1)S(1)}, bf16[768,512]{1,0:T(8,128)(2,1)}, u32[]{:S(2)}) copy-start(bf16[768,512]{1,0:T(8,128)(2,1)} %param.26) | copy-start | bytes 2359300
  7.2 89.2 %reduce-scatter.19.cloned.1.call-start = ((), (), s32[]{:S(2)}) async-start(), calls=%async_computation.16 | async-start | bytes 3932160 | tf_op jit(solution)/shard_map/reduce_scatter | solution.py:185
  31.0 130.6 %copy-start.1 = (bf16[1024,768]{1,0:T(8,128)(2,1)S(1)}, bf16[1024,768]{1,0:T(8,128)(2,1)}, u32[]{:S(2)}) copy-start(bf16[1024,768]{1,0:T(8,128)(2,1)} %param.18) | copy-start | bytes 4718596
  33.3 128.2 %all-gather.10.cloned.1.call-start = ((), (), s32[]{:S(2)}) async-start(), calls=%async_computation.17 | async-start | bytes 3932160 | tf_op jit(solution)/shard_map/all_gather | solution.py:186
  96.4 138.5 %reduce-scatter.21.cloned.1.call-start = ((), (), s32[]{:S(2)}) async-start(), calls=%async_computation.18 | async-start | bytes 3932160 | tf_op jit(solution)/shard_map/reduce_scatter | solution.py:228
  96.5 68.4 %copy-start.47 = (f32[768]{0:T(1024)}, f32[768]{0:T(1024)S(1)}, u32[]{:S(2)}) copy-start(f32[768]{0:T(1024)S(1)} %convert_element_type.102) | copy-start | bytes 9220
  96.5 71.2 %copy-start.62 = (pred[1024]{0:T(1024)(128)(4,1)}, pred[1024]{0:T(1024)(128)(4,1)S(1)}, u32[]{:S(2)}) copy-start(pred[1024]{0:T(1024)(128)(4,1)S(1)} %iota_compare_fusion.3) | copy-start | bytes 3076
  175.9 124.0 %all-gather.12.cloned.1.call-start = ((), (), s32[]{:S(2)}) async-start(), calls=%async_computation.19 | async-start | bytes 3932160 | tf_op jit(solution)/shard_map/all_gather | solution.py:229
  235.0 165.2 %reduce-scatter.23.cloned.1.call-start = ((), (), s32[]{:S(2)}) async-start(), calls=%async_computation.20 | async-start | bytes 3932160 | tf_op jit(solution)/shard_map/reduce_scatter | solution.py:260
  341.1 122.1 %reduce-scatter.15.cloned.1.call-start = ((), (), s32[]{:S(2)}) async-start(), calls=%async_computation.12 | async-start | bytes 3932160 | tf_op jit(solution)/shard_map/reduce_scatter | solution.py:181
  361.1 167.2 %copy-start.51 = (f32[768]{0:T(1024)S(1)}, f32[768]{0:T(1024)}, u32[]{:S(2)}) copy-start(f32[768]{0:T(1024)} %copy-done.50) | copy-start | bytes 9220
  361.1 167.2 %copy-start.53 = (f32[1024]{0:T(1024)S(1)}, f32[1024]{0:T(1024)}, u32[]{:S(2)}) copy-start(f32[1024]{0:T(1024)} %copy-done.52) | copy-start | bytes 12292
  361.2 167.1 %all-gather.14.cloned.1.call-start = ((), (), s32[]{:S(2)}) async-start(), calls=%async_computation.21 | async-start | bytes 3932160 | tf_op jit(solution)/shard_map/all_gather | solution.py:261
  400.1 131.2 %copy-start.57 = (f32[1024]{0:T(1024)S(1)}, f32[1024]{0:T(1024)}, u32[]{:S(2)}) copy-start(f32[1024]{0:T(1024)} %copy-done.56) | copy-start | bytes 12292
  400.1 191.9 %all-gather.6.cloned.1.call-start = ((), (), s32[]{:S(2)}) async-start(), calls=%async_computation.13 | async-start | bytes 3932160 | tf_op jit(solution)/shard_map/all_gather | solution.py:182
  463.2 203.9 %reduce-scatter.17.cloned.1.call-start = ((), (), s32[]{:S(2)}) async-start(), calls=%async_computation.14 | async-start | bytes 3932160 | tf_op jit(solution)/shard_map/reduce_scatter | solution.py:189
  608.0 97.1 %reduce-scatter.37.cloned.1.call-start = ((), (), s32[]{:S(2)}) async-start(), calls=%async_computation.28 | async-start | bytes 884736
  612.5 131.3 %all-gather.8.cloned.1.call-start = ((), (), s32[]{:S(2)}) async-start(), calls=%async_computation.15 | async-start | bytes 1966080 | tf_op jit(solution)/shard_map/all_gather | solution.py:200
  669.3 115.6 %reduce-scatter.35.cloned.1.call-start = ((), (), s32[]{:S(2)}) async-start(), calls=%async_computation.27 | async-start | bytes 1769472 | tf_op jit(solution)/shard_map/reduce_scatter | solution.py:238
  675.1 152.1 %reduce-scatter.31.cloned.1.call-start = ((), (), s32[]{:S(2)}) async-start(), calls=%async_computation.25 | async-start | bytes 1769472 | tf_op jit(solution)/shard_map/reduce_scatter | solution.py:235
  678.6 190.8 %reduce-scatter.33.cloned.1.call-start = ((), (), s32[]{:S(2)}) async-start(), calls=%async_computation.26 | async-start | bytes 1769472 | tf_op jit(solution)/shard_map/reduce_scatter | solution.py:236
  682.8 225.3 %reduce-scatter.29.cloned.1.call-start = ((), (), s32[]{:S(2)}) async-start(), calls=%async_computation.24 | async-start | bytes 884736 | tf_op jit(solution)/shard_map/reduce_scatter | solution.py:269
  684.4 262.2 %reduce-scatter.25.cloned.1.call-start = ((), (), s32[]{:S(2)}) async-start(), calls=%async_computation.22 | async-start | bytes 884736 | tf_op jit(solution)/shard_map/reduce_scatter | solution.py:267
  686.0 299.3 %reduce-scatter.27.cloned.1.call-start = ((), (), s32[]{:S(2)}) async-start(), calls=%async_computation.23 | async-start | bytes 884736 | tf_op jit(solution)/shard_map/reduce_scatter | solution.py:268
  (74 other events, 453.2 us)
Sparse Core Ops, SparseCore 0:
  33.4 62.9 reduce-scatter.18
  98.0 63.5 all-gather.9
  176.0 58.8 reduce-scatter.20
  236.4 63.5 all-gather.11
  341.2 58.8 reduce-scatter.22
  402.8 60.2 reduce-scatter.14
  464.7 63.5 all-gather.13
  529.9 62.1 all-gather.5
  608.1 58.8 reduce-scatter.16
  670.0 35.0 reduce-scatter.36
  706.7 37.0 all-gather.7
  747.5 37.3 reduce-scatter.34
  788.7 38.4 reduce-scatter.30
  831.0 38.4 reduce-scatter.32
  873.0 34.9 reduce-scatter.28
  911.6 34.9 reduce-scatter.24
  950.2 34.9 reduce-scatter.26
where the time goes:
time: 1000 us; the launch traced here: 995 us
  waiting for transfers between devices  815 us (82%)
  matrix products  75.7 us (8%)
  other arithmetic  32.9 us (3%)
  local copies, waits for them, and re-layouts  28 us (3%)
  between operations  16.9 us (2%)
  blocking collectives  12.6 us (1%)
  loops' own time  12.1 us (1%)
    all_gather x1, waiting for transfers between devices, body(): normed_one_back = lax.all_gather(normed_one_share, 'mp', axis=0, tiled=True)  65.1 us
    all_gather x1, waiting for transfers between devices, attention_repeat(): return lax.all_gather(share, 'mp', axis=0, tiled=True)  65 us
    all_gather x1, waiting for transfers between devices, body(): normed_two_back = lax.all_gather(normed_two_share, 'mp', axis=0, tiled=True)  64.4 us
    reduce_scatter x1, waiting for transfers between devices, attention_repeat(): lax.psum_scatter(partial_value, 'mp', scatter_dimension=0, tiled=True)  63 us
    reduce_scatter x1, waiting for transfers between devices, attention_total(): lax.psum_scatter(partial_value, 'mp', scatter_dimension=0, tiled=True)  63 us
    all_gather x1, waiting for transfers between devices, attention_total(): return lax.all_gather(share, 'mp', axis=0, tiled=True)  60.7 us
    reduce_scatter x1, waiting for transfers between devices, body(): lax.psum_scatter(normed_two_part, 'mp', scatter_dimension=0, tiled=True)  59 us
    reduce_scatter x1, waiting for transfers between devices, body(): lax.psum_scatter(jnp.dot(first_pass[10], down_weight, preferred_element_t...  54.5 us
  transfers between devices with their start and end apart: 17, of which 17 were waited for; matrix products, arithmetic and copies ran while one was open for 4% of the time, Pallas kernels for 0%

commit v1 on v0

--- a/solution.py
+++ b/solution.py
@@ -197,7 +197,14 @@
     hidden_here = lax.dynamic_slice_in_dim(first_pass[6], row_start, rows_here, 0)
     keep_here = lax.dynamic_slice_in_dim(row_keep, row_start, rows_here, 0)
     output_here = jnp.where(keep_here, hidden_here + feedforward_share, 0.0).astype(jnp.bfloat16)
-    layer_output = lax.all_gather(output_here, "mp", axis=0, tiled=True)
+    devices = lax.axis_size("mp")
+    hops = [(i, (i + 1) % devices) for i in range(devices)]
+    parts = [output_here]
+    for far in range(1, devices):
+        parts = [lax.ppermute(parts[0], "mp", hops), *parts]
+    out = jnp.concatenate(parts, axis=0)
+    shift = (lax.axis_index("mp") + 1) * parts[-1].shape[0]
+    layer_output = jnp.roll(out, shift, axis=0)
     saved = layer_forward(inputs, weights, valid_mask, attention_repeat)
     (
         normed_one,

time: 1000 us -> 964 us (0.964)
  waiting for transfers between devices: 815 us -> 773 us
    all_gather x1 -> x0, waiting for transfers between devices: 23.3 us -> none  [body(): layer_output = lax.all_gather(output_here, 'mp', axis=0, tiled=True)]
    ppermute x0 -> x3, waiting for transfers between devices: none -> 21.8 us  [body(): parts = [lax.ppermute(parts[0], 'mp', hops), *parts]]
    reduce_scatter x1, waiting for transfers between devices: 41.1 us -> 21.3 us  [body(): lax.psum_scatter(down_grad, 'dp', scatter_dimension=1, tiled=True)]
    reduce_scatter x1, waiting for transfers between devices: 54.5 us -> 40.5 us  [body(): lax.psum_scatter(jnp.dot(first_pass[10], down_weight, preferred_element_t...]
  transfers between devices with their start and end apart: 17 -> 19, of which waited for: 17 -> 18; matrix products, arithmetic and copies ran while one was open for 4% -> 5% of each run, Pallas kernels for 0% -> 0%
where the time goes in v1:
time: 964 us; the launch traced here: 955 us
  waiting for transfers between devices  773 us (80%)
  matrix products  74.5 us (8%)
  other arithmetic  32.1 us (3%)
  local copies, waits for them, and re-layouts  31.2 us (3%)
  between operations  17 us (2%)
  blocking collectives  12.7 us (1%)
  loops' own time  12.1 us (1%)
    all_gather x1, waiting for transfers between devices, body(): normed_one_back = lax.all_gather(normed_one_share, 'mp', axis=0, tiled=True)  65.1 us
    all_gather x1, waiting for transfers between devices, attention_repeat(): return lax.all_gather(share, 'mp', axis=0, tiled=True)  65 us
    all_gather x1, waiting for transfers between devices, body(): normed_two_back = lax.all_gather(normed_two_share, 'mp', axis=0, tiled=True)  64.4 us
    reduce_scatter x1, waiting for transfers between devices, attention_repeat(): lax.psum_scatter(partial_value, 'mp', scatter_dimension=0, tiled=True)  63 us
    reduce_scatter x1, waiting for transfers between devices, attention_total(): lax.psum_scatter(partial_value, 'mp', scatter_dimension=0, tiled=True)  63 us
    all_gather x1, waiting for transfers between devices, attention_total(): return lax.all_gather(share, 'mp', axis=0, tiled=True)  60.7 us
    reduce_scatter x1, waiting for transfers between devices, body(): lax.psum_scatter(normed_two_part, 'mp', scatter_dimension=0, tiled=True)  59 us
    reduce_scatter x1, waiting for transfers between devices, body(): lax.psum_scatter(up_grad, 'dp', scatter_dimension=0, tiled=True)  42.4 us
  transfers between devices with their start and end apart: 19, of which 18 were waited for; matrix products, arithmetic and copies ran while one was open for 5% of the time, Pallas kernels for 0%

profile of v1, /device:TPU:0, one launch (start us, length us, event | category | flops | bytes accessed | tf_op | source)
XLA Modules:
  0.0 954.9 jit_solution(3671255314510053442)
XLA Ops:
  16.5 12.8 %while.67 = (s32[]{:T(128)}, bf16[2,512,3,64]{1,3,2,0:T(8,128)(2,1)S(1)}, f32[2,3,512,1]{2,1,3,0:T(4,128)S(1)}, s32[2]{0:T(128)S(1)}, bf16[1024,3,64]{0,2,1:T(8,...) while((s32[]{:T(128)}, ...), condition=%wide.region_11.12_spmd.clone, body=%wide.region_8.11_spmd.clone.sunk | while | flops 415334912 | bytes 20129972 | solution.py:46
  33.4 63.0 %reduce-scatter.19.cloned.1.call-done = f32[256,768]{1,0:T(8,128)} async-done(((f32[1024,768]{1,0:T(8,128)}), f32[256,768]{1,0:T(8,128)}) %reduce-scatter.19.cloned.1.call-update) | async-done | bytes 786448 | tf_op jit(solution)/shard_map/reduce_scatter | solution.py:185
  96.6 65.0 %all-gather.7.cloned.1.call-done = f32[1024,768]{1,0:T(8,128)} async-done(((f32[256,768]{1,0:T(8,128)}), f32[1024,768]{1,0:T(8,128)}) %all-gather.7.cloned.1.call-update) | async-done | bytes 3145744 | tf_op jit(solution)/shard_map/all_gather | solution.py:186
  176.2 59.0 %reduce-scatter.21.cloned.1.call-done = f32[256,768]{1,0:T(8,128)} async-done(((f32[1024,768]{1,0:T(8,128)}), f32[256,768]{1,0:T(8,128)}) %reduce-scatter.21.cloned.1.call-update) | async-done | bytes 786448 | tf_op jit(solution)/shard_map/reduce_scatter | solution.py:235
  235.7 64.4 %all-gather.9.cloned.1.call-done = f32[1024,768]{1,0:T(8,128)} async-done(((f32[256,768]{1,0:T(8,128)}), f32[1024,768]{1,0:T(8,128)}) %all-gather.9.cloned.1.call-update) | async-done | bytes 3145744 | tf_op jit(solution)/shard_map/all_gather | solution.py:236
  310.8 25.0 %while.68 = (s32[]{:T(128)}, f32[1024,3,64]{0,2,1:T(8,128)S(1)}, f32[1024,3,64]{0,2,1:T(8,128)}, bf16[2,512,3,64]{1,3,2,0:T(8,128)(2,1)}, s32[2]{0:T(128)}, /*in...) while((s32[]{:T(128)}, f32[1024,3,64]{0,2,1:T(8,128)S(1)}, ...), condition=%wide.region_18.19_spmd.clone, body=%wide.region_16.18_spmd.clone.sunk | while | flops 1026392576 | bytes 66714016 | solution.py:83
  342.5 14.3 %while.66 = (s32[]{:T(128)}, bf16[2,512,3,64]{1,3,2,0:T(8,128)(2,1)}, s32[2]{0:T(128)S(1)}, bf16[1024,3,64]{0,2,1:T(8,128)(2,1)S(1)}, bf16[1024,3,64]{0,2,1:T(8,...) while((s32[]{:T(128)}, ...), condition=%wide.region_4.5_spmd.clone, body=%wide.region_1.4_spmd.clone.sunk | while | flops 415334912 | bytes 23261408 | solution.py:46
  361.6 38.9 %reduce-scatter.23.cloned.1.call-done = f32[256,768]{1,0:T(8,128)} async-done(((f32[1024,768]{1,0:T(8,128)}), f32[256,768]{1,0:T(8,128)}) %reduce-scatter.23.cloned.1.call-update) | async-done | bytes 786448 | tf_op jit(solution)/shard_map/reduce_scatter | solution.py:267
  400.6 63.0 %reduce-scatter.15.cloned.1.call-done = f32[256,768]{1,0:T(8,128)} async-done(((f32[1024,768]{1,0:T(8,128)}), f32[256,768]{1,0:T(8,128)}) %reduce-scatter.15.cloned.1.call-update) | async-done | bytes 786448 | tf_op jit(solution)/shard_map/reduce_scatter | solution.py:181
  463.6 65.1 %all-gather.11.cloned.1.call-done = f32[1024,768]{1,0:T(8,128)} async-done(((f32[256,768]{1,0:T(8,128)}), f32[1024,768]{1,0:T(8,128)}) %all-gather.11.cloned.1.call-update) | async-done | bytes 3145744 | tf_op jit(solution)/shard_map/all_gather | solution.py:268
  531.7 60.7 %all-gather.5.cloned.1.call-done = f32[1024,768]{1,0:T(8,128)} async-done(((f32[256,768]{1,0:T(8,128)}), f32[1024,768]{1,0:T(8,128)}) %all-gather.5.cloned.1.call-update) | async-done | bytes 3145744 | tf_op jit(solution)/shard_map/all_gather | solution.py:182
  602.0 6.2 fusion.72
  612.9 5.6 fusion.73
  626.9 40.5 %reduce-scatter.17.cloned.1.call-done = f32[256,768]{1,0:T(8,128)} async-done(((f32[1024,768]{1,0:T(8,128)}), f32[256,768]{1,0:T(8,128)}) %reduce-scatter.17.cloned.1.call-update) | async-done | bytes 786448 | tf_op jit(solution)/shard_map/reduce_scatter | solution.py:189
  671.5 10.0 %collective-permute-done = bf16[256,768]{1,0:T(8,128)(2,1)} collective-permute-done((bf16[256,768]{1,0:T(8,128)(2,1)S(1)}, bf16[256,768]{1,0:T(8,128)(2,1)}, u32[]{:S(2)}, u32[]{:S(2)}) %collective-permute-start) | collective-permute-done | bytes 393248 | tf_op jit(solution)/shard_map/ppermute | solution.py:204
  681.5 11.8 %collective-permute-done.1 = bf16[256,768]{1,0:T(8,128)(2,1)S(1)} collective-permute-done((bf16[256,768]{1,0:T(8,128)(2,1)}, bf16[256,768]{1,0:T(8,128)(2,1)S(1)}, u32[]{:S(2)}, u32[]{:S(2)}) %collective-permute-start.1) | collective-permute-done | bytes 393248 | tf_op jit(solution)/shard_map/ppermute | solution.py:204
  696.1 9.3 reduce-scatter.37.cloned.1.call-done
  707.0 12.7 %all-reduce.2 = (f32[768]{0:T(1024)S(1)}, f32[768]{0:T(1024)S(1)}) all-reduce(f32[768]{0:T(1024)S(1)} %get-tuple-element.302, f32[768]{0:T(1024)S(1)} %copy-done.61), channel_id=7, replica_groups=mesh['dp'=8,'mp'=4] {'dp'}, use_global_device_ids=true, to_apply=%region_22.23.clone | all-reduce | flops 1536 | bytes 12288
  726.5 21.3 %reduce-scatter.35.cloned.1.call-done = f32[512,96]{0,1:T(8,128)} async-done(((f32[512,768]{0,1:T(8,128)}), f32[512,96]{0,1:T(8,128)}) %reduce-scatter.35.cloned.1.call-update) | async-done | bytes 196624 | tf_op jit(solution)/shard_map/reduce_scatter | solution.py:245
  747.8 42.2 %reduce-scatter.31.cloned.1.call-done = f32[96,512]{1,0:T(8,128)} async-done(((f32[768,512]{1,0:T(8,128)}), f32[96,512]{1,0:T(8,128)}) %reduce-scatter.31.cloned.1.call-update) | async-done | bytes 196624 | tf_op jit(solution)/shard_map/reduce_scatter | solution.py:242
  790.0 42.4 %reduce-scatter.33.cloned.1.call-done = f32[96,512]{1,0:T(8,128)} async-done(((f32[768,512]{1,0:T(8,128)}), f32[96,512]{1,0:T(8,128)}) %reduce-scatter.33.cloned.1.call-update) | async-done | bytes 196624 | tf_op jit(solution)/shard_map/reduce_scatter | solution.py:243
  832.4 38.6 %reduce-scatter.29.cloned.1.call-done = f32[96,192]{1,0:T(8,128)} async-done(((f32[768,192]{1,0:T(8,128)}), f32[96,192]{1,0:T(8,128)}) %reduce-scatter.29.cloned.1.call-update) | async-done | bytes 73744 | tf_op jit(solution)/shard_map/reduce_scatter | solution.py:276
  870.9 38.6 %reduce-scatter.25.cloned.1.call-done = f32[96,192]{1,0:T(8,128)} async-done(((f32[768,192]{1,0:T(8,128)}), f32[96,192]{1,0:T(8,128)}) %reduce-scatter.25.cloned.1.call-update) | async-done | bytes 73744 | tf_op jit(solution)/shard_map/reduce_scatter | solution.py:274
  909.5 38.6 %reduce-scatter.27.cloned.1.call-done = f32[96,192]{1,0:T(8,128)} async-done(((f32[768,192]{1,0:T(8,128)}), f32[96,192]{1,0:T(8,128)}) %reduce-scatter.27.cloned.1.call-update) | async-done | bytes 73744 | tf_op jit(solution)/shard_map/reduce_scatter | solution.py:275
  (310 shorter events, 128.8 us)
Async XLA Ops:
  7.2 159.6 %copy-start = (bf16[768,512]{1,0:T(8,128)(2,1)S(1)}, bf16[768,512]{1,0:T(8,128)(2,1)}, u32[]{:S(2)}) copy-start(bf16[768,512]{1,0:T(8,128)(2,1)} %param.26) | copy-start | bytes 2359300
  7.2 89.3 %reduce-scatter.19.cloned.1.call-start = ((), (), s32[]{:S(2)}) async-start(), calls=%async_computation.15 | async-start | bytes 3932160 | tf_op jit(solution)/shard_map/reduce_scatter | solution.py:185
  31.1 130.6 %copy-start.1 = (bf16[1024,768]{1,0:T(8,128)(2,1)S(1)}, bf16[1024,768]{1,0:T(8,128)(2,1)}, u32[]{:S(2)}) copy-start(bf16[1024,768]{1,0:T(8,128)(2,1)} %param.18) | copy-start | bytes 4718596
  33.4 128.2 %all-gather.7.cloned.1.call-start = ((), (), s32[]{:S(2)}) async-start(), calls=%async_computation.16 | async-start | bytes 3932160 | tf_op jit(solution)/shard_map/all_gather | solution.py:186
  96.5 138.7 %reduce-scatter.21.cloned.1.call-start = ((), (), s32[]{:S(2)}) async-start(), calls=%async_computation.17 | async-start | bytes 3932160 | tf_op jit(solution)/shard_map/reduce_scatter | solution.py:235
  176.1 124.1 %all-gather.9.cloned.1.call-start = ((), (), s32[]{:S(2)}) async-start(), calls=%async_computation.18 | async-start | bytes 3932160 | tf_op jit(solution)/shard_map/all_gather | solution.py:236
  235.2 165.3 %reduce-scatter.23.cloned.1.call-start = ((), (), s32[]{:S(2)}) async-start(), calls=%async_computation.19 | async-start | bytes 3932160 | tf_op jit(solution)/shard_map/reduce_scatter | solution.py:267
  341.5 122.1 %reduce-scatter.15.cloned.1.call-start = ((), (), s32[]{:S(2)}) async-start(), calls=%async_computation.12 | async-start | bytes 3932160 | tf_op jit(solution)/shard_map/reduce_scatter | solution.py:181
  361.5 167.2 %copy-start.52 = (f32[768]{0:T(1024)S(1)}, f32[768]{0:T(1024)}, u32[]{:S(2)}) copy-start(f32[768]{0:T(1024)} %copy-done.51) | copy-start | bytes 9220
  361.6 167.2 %copy-start.54 = (f32[1024]{0:T(1024)S(1)}, f32[1024]{0:T(1024)}, u32[]{:S(2)}) copy-start(f32[1024]{0:T(1024)} %copy-done.53) | copy-start | bytes 12292
  361.6 167.1 %all-gather.11.cloned.1.call-start = ((), (), s32[]{:S(2)}) async-start(), calls=%async_computation.20 | async-start | bytes 3932160 | tf_op jit(solution)/shard_map/all_gather | solution.py:268
  400.5 131.2 %copy-start.58 = (f32[1024]{0:T(1024)S(1)}, f32[1024]{0:T(1024)}, u32[]{:S(2)}) copy-start(f32[1024]{0:T(1024)} %copy-done.57) | copy-start | bytes 12292
  400.5 191.9 %all-gather.5.cloned.1.call-start = ((), (), s32[]{:S(2)}) async-start(), calls=%async_computation.13 | async-start | bytes 3932160 | tf_op jit(solution)/shard_map/all_gather | solution.py:182
  463.6 203.8 %reduce-scatter.17.cloned.1.call-start = ((), (), s32[]{:S(2)}) async-start(), calls=%async_computation.14 | async-start | bytes 3932160 | tf_op jit(solution)/shard_map/reduce_scatter | solution.py:189
  608.3 97.1 %reduce-scatter.37.cloned.1.call-start = ((), (), s32[]{:S(2)}) async-start(), calls=%async_computation.27 | async-start | bytes 884736
  612.8 135.0 %reduce-scatter.35.cloned.1.call-start = ((), (), s32[]{:S(2)}) async-start(), calls=%async_computation.26 | async-start | bytes 1769472 | tf_op jit(solution)/shard_map/reduce_scatter | solution.py:245
  618.6 171.5 %reduce-scatter.31.cloned.1.call-start = ((), (), s32[]{:S(2)}) async-start(), calls=%async_computation.24 | async-start | bytes 1769472 | tf_op jit(solution)/shard_map/reduce_scatter | solution.py:242
  621.1 211.3 %reduce-scatter.33.cloned.1.call-start = ((), (), s32[]{:S(2)}) async-start(), calls=%async_computation.25 | async-start | bytes 1769472 | tf_op jit(solution)/shard_map/reduce_scatter | solution.py:243
  625.2 245.8 %reduce-scatter.29.cloned.1.call-start = ((), (), s32[]{:S(2)}) async-start(), calls=%async_computation.23 | async-start | bytes 884736 | tf_op jit(solution)/shard_map/reduce_scatter | solution.py:276
  626.8 282.7 %reduce-scatter.25.cloned.1.call-start = ((), (), s32[]{:S(2)}) async-start(), calls=%async_computation.21 | async-start | bytes 884736 | tf_op jit(solution)/shard_map/reduce_scatter | solution.py:274
  668.9 12.7 %collective-permute-start = (bf16[256,768]{1,0:T(8,128)(2,1)S(1)}, bf16[256,768]{1,0:T(8,128)(2,1)}, u32[]{:S(2)}, u32[]{:S(2)}) collective-permute-start(bf16[256,768]{1,0:T(8,128)(2,1)S(1)} %select_convert_fusion), channel_id=1, source_target_pairs={{0,1},{1,2},{2,3},{3,0},{4,5},{5,6},{6,7},{7,4},{8,9},{9,10},{10,1... | collective-permute-start | bytes 1179656 | tf_op jit(solution)/shard_map/ppermute | solution.py:204
  671.4 276.7 %reduce-scatter.27.cloned.1.call-start = ((), (), s32[]{:S(2)}) async-start(), calls=%async_computation.22 | async-start | bytes 884736 | tf_op jit(solution)/shard_map/reduce_scatter | solution.py:275
  681.5 11.8 %collective-permute-start.1 = (bf16[256,768]{1,0:T(8,128)(2,1)}, bf16[256,768]{1,0:T(8,128)(2,1)S(1)}, u32[]{:S(2)}, u32[]{:S(2)}) collective-permute-start(bf16[256,768]{1,0:T(8,128)(2,1)} %collective-permute-done), channel_id=1, source_target_pairs={{0,1},{1,2},{2,3},{3,0},{4,5},{5,6},{6,7},{7,4},{8,9},{9,10},{10,1... | collective-permute-start | bytes 1179656 | tf_op jit(solution)/shard_map/ppermute | solution.py:204
  693.3 27.6 %collective-permute-start.2 = (bf16[256,768]{1,0:T(8,128)(2,1)S(1)}, bf16[256,768]{1,0:T(8,128)(2,1)}, u32[]{:S(2)}, u32[]{:S(2)}) collective-permute-start(bf16[256,768]{1,0:T(8,128)(2,1)S(1)} %collective-permute-done.1), channel_id=1, source_target_pairs={{0,1},{1,2},{2,3},{3,0},{4,5},{5,6},{6,7},{7,4},{8,9},{9,10},{10,1... | collective-permute-start | bytes 1179656 | tf_op jit(solution)/shard_map/ppermute | solution.py:204
  (77 other events, 728.9 us)
Sparse Core Ops, SparseCore 0:
  33.5 62.9 reduce-scatter.18
  98.1 63.5 all-gather.6
  176.2 58.8 reduce-scatter.20
  236.6 63.5 all-gather.8
  341.6 58.8 reduce-scatter.22
  403.3 60.2 reduce-scatter.14
  465.1 63.5 all-gather.10
  530.3 62.1 all-gather.4
  608.4 58.8 reduce-scatter.16
  670.4 35.0 reduce-scatter.36
  709.3 38.4 reduce-scatter.34
  751.5 38.4 reduce-scatter.30
  793.9 38.4 reduce-scatter.32
  835.9 34.9 reduce-scatter.28
  874.5 34.9 reduce-scatter.24
  913.1 34.9 reduce-scatter.26
